TPU v7x, 32 devices: a whole 2x2x4 slice. The times are simulated.
32 devices in a mesh: blk: 16 (over z, y, x), grp: 2 (over core).
Axes of the slice: x: 2, y: 2, z: 4, core: 2. Of those that a mesh axis runs over, the one named last changes fastest.
Arguments:
- schur_blocks: bfloat16 [64, 1024, 1024], P(('blk', 'grp')), may hold values from -1 to 5, as said below
- residual: float32 [64, 1024, 128], P(('blk', 'grp')), may hold values from -200 to 200
- direction: float32 [64, 1024, 128], P(('blk', 'grp')), may hold values from -200 to 200
- corner_map: int32 [64, 24], P(('blk', 'grp')), may hold values from 0 to 511
- panel_order: int32 [8], replicated, may hold values from 0 to 7, each once
- coarse_factor: float32 [8, 8, 1024, 1024], P(None, None, 'blk'), may hold values from -0.0625 to 0.0625
- block_inverses: float32 [8, 1024, 1024], P(None, 'blk'), may hold values from -0.1875 to 0.1875
Outputs:
- residual_next: float32 [64, 1024, 128], P(('blk', 'grp'))
- direction_next: float32 [64, 1024, 128], P(('blk', 'grp'))
Inputs may be any that keep to these rules, and one draw needn't show every extreme that they name: `schur_blocks`: each subdomain's block is symmetric positive definite. `panel_order`: each coarse block appears once.
All inputs are finite; a program needn't handle non-finite values.
Results may differ from a plain program's by a relative error of at most 0.0048.
Values sent between devices are 32-bit elements; how exact they have to be, the bound alone decides.
No kernel may reach another device: no remote copies, remote signals or barrier semaphores. Data moves between devices by JAX's collectives and lax.ppermute only.
A program may use at most 64 MiB of HBM per device.

v0:
```python
import jax
import jax.numpy as jnp
from jax import lax
from jax.sharding import PartitionSpec as P

PANELS = 8
precise = lax.Precision.HIGHEST


def squares(residual):
    return lax.psum(jnp.sum(residual * residual, axis=(0, 1)), ("blk", "grp"))


def solve(coarse, panel_order, coarse_factor, block_inverses):
    pending = jnp.zeros_like(coarse)
    solved = jnp.zeros_like(coarse)
    for position in range(PANELS):
        current = panel_order[position]
        target = lax.dynamic_index_in_dim(coarse - pending, current, 0, keepdims=False)
        inverse = lax.dynamic_index_in_dim(block_inverses, current, 0, keepdims=False)
        block_value = jnp.dot(
            inverse,
            lax.all_gather(target, "blk", axis=0, tiled=True),
            precision=precise,
            preferred_element_type=jnp.float32,
        )
        solved = lax.dynamic_update_index_in_dim(solved, block_value, current, 0)
        if position + 1 < PANELS:
            coupling = lax.dynamic_index_in_dim(coarse_factor, current, 1, keepdims=False)
            pending = pending + jnp.einsum(
                "aic,cv->aiv",
                coupling,
                lax.all_gather(block_value, "blk", axis=0, tiled=True),
                precision=precise,
            )
    return solved


def local(
    schur_blocks, residual, direction, corner_map, panel_order, coarse_factor, block_inverses
):
    panels = block_inverses.shape[0]
    rows_b = block_inverses.shape[1]
    sub_count = schur_blocks.shape[0]
    corners = corner_map.shape[1]
    columns_iota = lax.broadcasted_iota(jnp.int32, (sub_count, corners, panels * rows_b), 2)
    placing = (corner_map[:, :, None] == columns_iota).astype(jnp.float32)
    norm_now = squares(residual)
    applied = jnp.einsum(
        "sij,sjv->siv",
        schur_blocks,
        direction.astype(jnp.bfloat16),
        preferred_element_type=jnp.float32,
    )
    curvature = lax.psum(jnp.sum(direction * applied, axis=(0, 1)), ("blk", "grp"))
    step_size = norm_now / curvature
    residual = residual - step_size * applied
    norm_next = squares(residual)
    corner_part = jnp.einsum("scm,scv->mv", placing, residual[:, :corners, :], precision=precise)
    corner_part = corner_part.reshape(panels, rows_b, -1)
    coarse_part = lax.psum(corner_part, "grp")
    solved = solve(coarse_part, panel_order, coarse_factor, block_inverses)
    flat_solved = solved.reshape(panels * rows_b, -1)
    correction = jnp.einsum("scm,mv->scv", placing, flat_solved, precision=precise)
    corrected = jnp.concatenate(
        [residual[:, :corners, :] + correction, residual[:, corners:, :]], axis=1
    )
    direction = corrected + norm_next / norm_now * direction
    return (residual, direction)


def solution(mesh):
    in_specs = (
        P(("blk", "grp"), None, None),
        P(("blk", "grp"), None, None),
        P(("blk", "grp"), None, None),
        P(("blk", "grp"), None),
        P(),
        P(None, None, "blk", None),
        P(None, "blk", None),
    )
    out_specs = (P(("blk", "grp"), None, None), P(("blk", "grp"), None, None))
    return jax.shard_map(local, mesh=mesh, in_specs=in_specs, out_specs=out_specs, check_vma=False)
```

profile of v0, /device:TPU:0, one launch (start us, length us, event | category | flops | bytes accessed | tf_op | source)
XLA Modules:
  0.0 743.4 jit_solution(7819238958384494164)
XLA Ops:
  8.9 5.0 multiply_reduce_fusion.1
  13.9 41.9 %all-reduce = (f32[128]{0:T(128)S(1)}, f32[128]{0:T(128)S(1)}) all-reduce(f32[128]{0:T(128)S(1)} %multiply_reduce_fusion.2, f32[128]{0:T(128)S(1)} %get-tuple-element.14), channel_id=1, replica_groups=mesh['blk'=16,'grp'=2] {'blk','grp'}, use_global_device_ids=true, to_apply=%region_1.0 | all-reduce | flops 256 | bytes 2048 | tf_op jit(solution)/shard_map/psum | solution.py:11
  55.8 1.8 multiply_reduce_fusion
  70.6 40.0 %psum.31 = f32[128]{0:T(128)S(1)} all-reduce(f32[128]{0:T(128)S(1)} %get-tuple-element.4), channel_id=1, replica_groups=mesh['blk'=16,'grp'=2] {'blk','grp'}, use_global_device_ids=true, to_apply=%region_6.0 | all-reduce | flops 128 | bytes 1024 | tf_op jit(solution)/shard_map/psum | solution.py:11
  116.4 43.7 %all-gather = f32[1,1024,128]{2,1,0:T(8,128)S(1)} all-gather(f32[1,64,128]{2,1,0:T(8,128)S(1)} %constant_dynamic-slice_fusion), channel_id=2, replica_groups=mesh['blk'=16,'grp'=2] {'blk'}, dimensions={1}, use_global_device_ids=true | all-gather | bytes 557056 | tf_op jit(solution)/shard_map/all_gather | solution.py:23
  160.7 38.5 %all_gather.46 = f32[1024,128]{1,0:T(8,128)S(1)} all-gather(f32[64,128]{1,0:T(8,128)S(1)} %get-tuple-element.17), channel_id=1, replica_groups=mesh['blk'=16,'grp'=2] {'blk'}, dimensions={0}, use_global_device_ids=true | all-gather | bytes 557056 | tf_op jit(solution)/shard_map/all_gather | solution.py:33
  199.2 3.4 fusion.12
  202.6 40.7 %all-gather.1 = f32[1,1024,128]{2,1,0:T(8,128)S(1)} all-gather(f32[1,64,128]{2,1,0:T(8,128)S(1)} %dynamic-slice_subtract_fusion.6), channel_id=3, replica_groups=mesh['blk'=16,'grp'=2] {'blk'}, dimensions={1}, use_global_device_ids=true | all-gather | bytes 557056 | tf_op jit(solution)/shard_map/all_gather | solution.py:23
  243.8 38.6 %all_gather.48 = f32[1024,128]{1,0:T(8,128)S(1)} all-gather(f32[64,128]{1,0:T(8,128)S(1)} %get-tuple-element.19), channel_id=1, replica_groups=mesh['blk'=16,'grp'=2] {'blk'}, dimensions={0}, use_global_device_ids=true | all-gather | bytes 557056 | tf_op jit(solution)/shard_map/all_gather | solution.py:33
  282.4 3.4 fusion.21
  285.8 40.3 %all-gather.2 = f32[1,1024,128]{2,1,0:T(8,128)S(1)} all-gather(f32[1,64,128]{2,1,0:T(8,128)S(1)} %dynamic-slice_subtract_fusion.5), channel_id=4, replica_groups=mesh['blk'=16,'grp'=2] {'blk'}, dimensions={1}, use_global_device_ids=true | all-gather | bytes 557056 | tf_op jit(solution)/shard_map/all_gather | solution.py:23
  326.6 38.6 %all_gather.50 = f32[1024,128]{1,0:T(8,128)S(1)} all-gather(f32[64,128]{1,0:T(8,128)S(1)} %get-tuple-element.21), channel_id=1, replica_groups=mesh['blk'=16,'grp'=2] {'blk'}, dimensions={0}, use_global_device_ids=true | all-gather | bytes 557056 | tf_op jit(solution)/shard_map/all_gather | solution.py:33
  365.2 3.4 fusion.24
  368.6 41.1 %all-gather.3 = f32[1,1024,128]{2,1,0:T(8,128)S(1)} all-gather(f32[1,64,128]{2,1,0:T(8,128)S(1)} %dynamic-slice_subtract_fusion.4), channel_id=5, replica_groups=mesh['blk'=16,'grp'=2] {'blk'}, dimensions={1}, use_global_device_ids=true | all-gather | bytes 557056 | tf_op jit(solution)/shard_map/all_gather | solution.py:23
  410.2 38.3 %all_gather.52 = f32[1024,128]{1,0:T(8,128)S(1)} all-gather(f32[64,128]{1,0:T(8,128)S(1)} %get-tuple-element.23), channel_id=1, replica_groups=mesh['blk'=16,'grp'=2] {'blk'}, dimensions={0}, use_global_device_ids=true | all-gather | bytes 557056 | tf_op jit(solution)/shard_map/all_gather | solution.py:33
  450.3 40.8 %all-gather.4 = f32[1,1024,128]{2,1,0:T(8,128)S(1)} all-gather(f32[1,64,128]{2,1,0:T(8,128)S(1)} %dynamic-slice_subtract_fusion.3), channel_id=6, replica_groups=mesh['blk'=16,'grp'=2] {'blk'}, dimensions={1}, use_global_device_ids=true | all-gather | bytes 557056 | tf_op jit(solution)/shard_map/all_gather | solution.py:23
  491.6 38.6 %all_gather.54 = f32[1024,128]{1,0:T(8,128)S(1)} all-gather(f32[64,128]{1,0:T(8,128)S(1)} %get-tuple-element.25), channel_id=1, replica_groups=mesh['blk'=16,'grp'=2] {'blk'}, dimensions={0}, use_global_device_ids=true | all-gather | bytes 557056 | tf_op jit(solution)/shard_map/all_gather | solution.py:33
  530.2 1.8 fusion.30
  532.0 40.5 %all-gather.5 = f32[1,1024,128]{2,1,0:T(8,128)S(1)} all-gather(f32[1,64,128]{2,1,0:T(8,128)S(1)} %dynamic-slice_subtract_fusion.2), channel_id=7, replica_groups=mesh['blk'=16,'grp'=2] {'blk'}, dimensions={1}, use_global_device_ids=true | all-gather | bytes 557056 | tf_op jit(solution)/shard_map/all_gather | solution.py:23
  573.0 38.5 %all_gather.56 = f32[1024,128]{1,0:T(8,128)S(1)} all-gather(f32[64,128]{1,0:T(8,128)S(1)} %get-tuple-element.27), channel_id=1, replica_groups=mesh['blk'=16,'grp'=2] {'blk'}, dimensions={0}, use_global_device_ids=true | all-gather | bytes 557056 | tf_op jit(solution)/shard_map/all_gather | solution.py:33
  613.3 40.4 %all-gather.6 = f32[1,1024,128]{2,1,0:T(8,128)S(1)} all-gather(f32[1,64,128]{2,1,0:T(8,128)S(1)} %dynamic-slice_subtract_fusion.1), channel_id=8, replica_groups=mesh['blk'=16,'grp'=2] {'blk'}, dimensions={1}, use_global_device_ids=true | all-gather | bytes 557056 | tf_op jit(solution)/shard_map/all_gather | solution.py:23
  654.1 38.3 %all_gather.58 = f32[1024,128]{1,0:T(8,128)S(1)} all-gather(f32[64,128]{1,0:T(8,128)S(1)} %get-tuple-element.29), channel_id=1, replica_groups=mesh['blk'=16,'grp'=2] {'blk'}, dimensions={0}, use_global_device_ids=true | all-gather | bytes 557056 | tf_op jit(solution)/shard_map/all_gather | solution.py:33
  692.4 1.8 fusion
  694.2 40.5 %all-gather.7 = f32[1,1024,128]{2,1,0:T(8,128)S(1)} all-gather(f32[1,64,128]{2,1,0:T(8,128)S(1)} %dynamic-slice_subtract_fusion), channel_id=9, replica_groups=mesh['blk'=16,'grp'=2] {'blk'}, dimensions={1}, use_global_device_ids=true | all-gather | bytes 557056 | tf_op jit(solution)/shard_map/all_gather | solution.py:23
  (46 shorter events, 14.0 us)
Async XLA Ops:
  7.2 153.0 %copy-start = (f32[8,64,1024]{2,1,0:T(8,128)S(1)}, f32[8,64,1024]{2,1,0:T(8,128)}, u32[]{:S(2)}) copy-start(f32[8,64,1024]{2,1,0:T(8,128)} %param.13) | copy-start | bytes 6291460
  7.2 108.5 %all-reduce.3.cloned.1.call-start = ((), (), s32[]{:S(2)}) async-start(), calls=%async_computation | async-start | bytes 524288 | tf_op jit(solution)/shard_map/psum | solution.py:61
  13.9 43.8 %copy-start.7 = (s32[2,24]{1,0:T(2,128)S(1)}, s32[2,24]{1,0:T(2,128)}, u32[]{:S(2)}) copy-start(s32[2,24]{1,0:T(2,128)} %param.10) | copy-start | bytes 580
  13.9 45.0 %copy-start.6 = (s32[8]{0:T(128)S(1)}, s32[8]{0:T(128)}, u32[]{:S(2)}) copy-start(s32[8]{0:T(128)} %param.11) | copy-start | bytes 100
  57.6 677.5 %copy-start.2 = (f32[2,1024,128]{2,1,0:T(8,128)}, f32[2,1024,128]{2,1,0:T(8,128)S(1)}, u32[]{:S(2)}) copy-start(f32[2,1024,128]{2,1,0:T(8,128)S(1)} %get-tuple-element.5) | copy-start | bytes 3145732
  160.2 42.4 %copy-start.5 = (f32[8,64,128]{2,1,0:T(8,128)S(1)}, f32[8,64,128]{2,1,0:T(8,128)}, u32[]{:S(2)}) copy-start(f32[8,64,128]{2,1,0:T(8,128)} %all-reduce.3.cloned.1.call-done) | copy-start | bytes 786436
  160.2 288.3 %copy-start.1 = (f32[8,8,64,1024]{3,2,1,0:T(8,128)S(1)}, f32[8,8,64,1024]{3,2,1,0:T(8,128)}, u32[]{:S(2)}) copy-start(f32[8,8,64,1024]{3,2,1,0:T(8,128)} %param.12) | copy-start | bytes 50331652
  692.4 43.1 %copy-start.3 = (f32[2,1024,128]{2,1,0:T(8,128)S(1)}, f32[2,1024,128]{2,1,0:T(8,128)}, u32[]{:S(2)}) copy-start(f32[2,1024,128]{2,1,0:T(8,128)} %param.9) | copy-start | bytes 3145732
  692.4 43.1 %copy-start.4 = (f32[2,1000,128]{2,1,0:T(8,128)S(1)}, f32[2,1000,128]{2,1,0:T(8,128)}, u32[]{:S(2)}) copy-start(f32[2,1000,128]{2,1,0:T(8,128)} %slice.42) | copy-start | bytes 3072004
Sparse Core Ops, SparseCore 0:
  59.0 18.0 all-reduce.2
where the time goes:
time: 744 us; the launch traced here: 743 us
  blocking collectives  679 us (91%)
  between operations  29.3 us (4%)
  matrix products  27.4 us (4%)
    all_gather x8, blocking collectives, solve(): lax.all_gather(target, 'blk', axis=0, tiled=True)  328 us
    all_gather x7, blocking collectives, solve(): lax.all_gather(block_value, 'blk', axis=0, tiled=True)  269 us
    psum x2, blocking collectives, squares(): return lax.psum(jnp.sum(residual * residual, axis=(0, 1)), ('blk', 'grp'))  82 us
    dot_general x7, matrix products, solve(): jnp.einsum('aic,cv->aiv', coupling, lax.all_gather(block_value, 'blk', ax...  17.4 us
  transfers between devices with their start and end apart: 1, of which 0 were waited for; matrix products, arithmetic and copies ran while one was open for 0% of the time, Pallas kernels for 0%

commit v1 on v0

--- a/solution.py
+++ b/solution.py
@@ -8,7 +8,9 @@
 
 
 def squares(residual):
-    return lax.psum(jnp.sum(residual * residual, axis=(0, 1)), ("blk", "grp"))
+    return jnp.sum(
+        lax.all_gather(jnp.sum(residual * residual, axis=(0, 1)), ("blk", "grp")), axis=0
+    )
 
 
 def solve(coarse, panel_order, coarse_factor, block_inverses):

time: 744 us -> 778 us (1.046)
  blocking collectives: 679 us -> 713 us
    all_gather x0 -> x2, blocking collectives: none -> 83.5 us  [squares(): lax.all_gather(jnp.sum(residual * residual, axis=(0, 1)), ('blk', 'grp'))]
    psum x2 -> x1, blocking collectives: 82 us -> 36.8 us  [local(): lax.psum(jnp.sum(direction * applied, axis=(0, 1)), ('blk', 'grp'))]
    all_gather x8, blocking collectives: 328 us -> 308 us  [solve(): lax.all_gather(target, 'blk', axis=0, tiled=True)]
    all_gather x7, blocking collectives: 269 us -> 285 us  [solve(): lax.all_gather(block_value, 'blk', axis=0, tiled=True)]
where the time goes in v1:
time: 778 us; the launch traced here: 777 us
  blocking collectives  713 us (92%)
  between operations  29 us (4%)
  matrix products  27.4 us (4%)
    all_gather x8, blocking collectives, solve(): lax.all_gather(target, 'blk', axis=0, tiled=True)  308 us
    all_gather x7, blocking collectives, solve(): lax.all_gather(block_value, 'blk', axis=0, tiled=True)  285 us
    all_gather x2, blocking collectives, squares(): lax.all_gather(jnp.sum(residual * residual, axis=(0, 1)), ('blk', 'grp'))  83.5 us
    psum x1, blocking collectives, local(): lax.psum(jnp.sum(direction * applied, axis=(0, 1)), ('blk', 'grp'))  36.8 us
    dot_general x7, matrix products, solve(): jnp.einsum('aic,cv->aiv', coupling, lax.all_gather(block_value, 'blk', ax...  17.4 us
  transfers between devices with their start and end apart: 1, of which 0 were waited for; matrix products, arithmetic and copies ran while one was open for 0% of the time, Pallas kernels for 0%

profile of v1, /device:TPU:0, one launch (start us, length us, event | category | flops | bytes accessed | tf_op | source)
XLA Modules:
  0.0 777.2 jit_solution(5588972585734248209)
XLA Ops:
  8.9 43.3 %all-gather.10 = f32[32,1,128]{2,1,0:T(1,128)S(1)} all-gather(f32[1,1,128]{2,1,0:T(1,128)S(1)} %bitcast.167), channel_id=2, replica_groups=mesh['blk'=16,'grp'=2] {'blk','grp'}, dimensions={0}, use_global_device_ids=true | all-gather | bytes 16896 | tf_op jit(solution)/shard_map/all_gather | solution.py:12
  52.2 5.0 multiply_reduce_fusion.1
  57.2 36.8 %psum.14 = f32[128]{0:T(128)S(1)} all-reduce(f32[128]{0:T(128)S(1)} %get-tuple-element.12), channel_id=1, replica_groups=mesh['blk'=16,'grp'=2] {'blk','grp'}, use_global_device_ids=true, to_apply=%region_3.0 | all-reduce | flops 128 | bytes 1024 | tf_op jit(solution)/shard_map/psum | solution.py:57
  94.0 1.8 multiply_reduce_fusion
  108.6 40.2 %all-gather.11 = f32[32,1,128]{2,1,0:T(1,128)S(1)} all-gather(f32[1,1,128]{2,1,0:T(1,128)S(1)} %bitcast.166), channel_id=11, replica_groups=mesh['blk'=16,'grp'=2] {'blk','grp'}, dimensions={0}, use_global_device_ids=true | all-gather | bytes 16896 | tf_op jit(solution)/shard_map/all_gather | solution.py:12
  154.5 38.3 %all-gather.1 = f32[1,1024,128]{2,1,0:T(8,128)S(1)} all-gather(f32[1,64,128]{2,1,0:T(8,128)S(1)} %constant_dynamic-slice_fusion), channel_id=3, replica_groups=mesh['blk'=16,'grp'=2] {'blk'}, dimensions={1}, use_global_device_ids=true | all-gather | bytes 557056 | tf_op jit(solution)/shard_map/all_gather | solution.py:25
  193.4 41.0 %all_gather.60 = f32[1024,128]{1,0:T(8,128)S(1)} all-gather(f32[64,128]{1,0:T(8,128)S(1)} %get-tuple-element.15), channel_id=1, replica_groups=mesh['blk'=16,'grp'=2] {'blk'}, dimensions={0}, use_global_device_ids=true | all-gather | bytes 557056 | tf_op jit(solution)/shard_map/all_gather | solution.py:35
  234.4 3.4 fusion.12
  237.8 38.5 %all-gather.2 = f32[1,1024,128]{2,1,0:T(8,128)S(1)} all-gather(f32[1,64,128]{2,1,0:T(8,128)S(1)} %dynamic-slice_subtract_fusion.6), channel_id=4, replica_groups=mesh['blk'=16,'grp'=2] {'blk'}, dimensions={1}, use_global_device_ids=true | all-gather | bytes 557056 | tf_op jit(solution)/shard_map/all_gather | solution.py:25
  276.8 41.2 %all_gather.62 = f32[1024,128]{1,0:T(8,128)S(1)} all-gather(f32[64,128]{1,0:T(8,128)S(1)} %get-tuple-element.17), channel_id=1, replica_groups=mesh['blk'=16,'grp'=2] {'blk'}, dimensions={0}, use_global_device_ids=true | all-gather | bytes 557056 | tf_op jit(solution)/shard_map/all_gather | solution.py:35
  318.0 3.4 fusion.21
  321.4 38.5 %all-gather.3 = f32[1,1024,128]{2,1,0:T(8,128)S(1)} all-gather(f32[1,64,128]{2,1,0:T(8,128)S(1)} %dynamic-slice_subtract_fusion.5), channel_id=5, replica_groups=mesh['blk'=16,'grp'=2] {'blk'}, dimensions={1}, use_global_device_ids=true | all-gather | bytes 557056 | tf_op jit(solution)/shard_map/all_gather | solution.py:25
  360.4 40.4 %all_gather.64 = f32[1024,128]{1,0:T(8,128)S(1)} all-gather(f32[64,128]{1,0:T(8,128)S(1)} %get-tuple-element.19), channel_id=1, replica_groups=mesh['blk'=16,'grp'=2] {'blk'}, dimensions={0}, use_global_device_ids=true | all-gather | bytes 557056 | tf_op jit(solution)/shard_map/all_gather | solution.py:35
  400.8 3.4 fusion.24
  404.2 38.7 %all-gather.4 = f32[1,1024,128]{2,1,0:T(8,128)S(1)} all-gather(f32[1,64,128]{2,1,0:T(8,128)S(1)} %dynamic-slice_subtract_fusion.4), channel_id=6, replica_groups=mesh['blk'=16,'grp'=2] {'blk'}, dimensions={1}, use_global_device_ids=true | all-gather | bytes 557056 | tf_op jit(solution)/shard_map/all_gather | solution.py:25
  443.3 40.5 %all_gather.66 = f32[1024,128]{1,0:T(8,128)S(1)} all-gather(f32[64,128]{1,0:T(8,128)S(1)} %get-tuple-element.21), channel_id=1, replica_groups=mesh['blk'=16,'grp'=2] {'blk'}, dimensions={0}, use_global_device_ids=true | all-gather | bytes 557056 | tf_op jit(solution)/shard_map/all_gather | solution.py:35
  483.9 1.8 fusion.27
  485.7 38.6 %all-gather.5 = f32[1,1024,128]{2,1,0:T(8,128)S(1)} all-gather(f32[1,64,128]{2,1,0:T(8,128)S(1)} %dynamic-slice_subtract_fusion.3), channel_id=7, replica_groups=mesh['blk'=16,'grp'=2] {'blk'}, dimensions={1}, use_global_device_ids=true | all-gather | bytes 557056 | tf_op jit(solution)/shard_map/all_gather | solution.py:25
  524.7 40.5 %all_gather.68 = f32[1024,128]{1,0:T(8,128)S(1)} all-gather(f32[64,128]{1,0:T(8,128)S(1)} %get-tuple-element.23), channel_id=1, replica_groups=mesh['blk'=16,'grp'=2] {'blk'}, dimensions={0}, use_global_device_ids=true | all-gather | bytes 557056 | tf_op jit(solution)/shard_map/all_gather | solution.py:35
  567.0 38.9 %all-gather.6 = f32[1,1024,128]{2,1,0:T(8,128)S(1)} all-gather(f32[1,64,128]{2,1,0:T(8,128)S(1)} %dynamic-slice_subtract_fusion.2), channel_id=8, replica_groups=mesh['blk'=16,'grp'=2] {'blk'}, dimensions={1}, use_global_device_ids=true | all-gather | bytes 557056 | tf_op jit(solution)/shard_map/all_gather | solution.py:25
  606.4 41.1 %all_gather.70 = f32[1024,128]{1,0:T(8,128)S(1)} all-gather(f32[64,128]{1,0:T(8,128)S(1)} %get-tuple-element.25), channel_id=1, replica_groups=mesh['blk'=16,'grp'=2] {'blk'}, dimensions={0}, use_global_device_ids=true | all-gather | bytes 557056 | tf_op jit(solution)/shard_map/all_gather | solution.py:35
  649.2 38.3 %all-gather.7 = f32[1,1024,128]{2,1,0:T(8,128)S(1)} all-gather(f32[1,64,128]{2,1,0:T(8,128)S(1)} %dynamic-slice_subtract_fusion.1), channel_id=9, replica_groups=mesh['blk'=16,'grp'=2] {'blk'}, dimensions={1}, use_global_device_ids=true | all-gather | bytes 557056 | tf_op jit(solution)/shard_map/all_gather | solution.py:25
  688.0 40.5 %all_gather.72 = f32[1024,128]{1,0:T(8,128)S(1)} all-gather(f32[64,128]{1,0:T(8,128)S(1)} %get-tuple-element.27), channel_id=1, replica_groups=mesh['blk'=16,'grp'=2] {'blk'}, dimensions={0}, use_global_device_ids=true | all-gather | bytes 557056 | tf_op jit(solution)/shard_map/all_gather | solution.py:35
  730.3 38.3 %all-gather.8 = f32[1,1024,128]{2,1,0:T(8,128)S(1)} all-gather(f32[1,64,128]{2,1,0:T(8,128)S(1)} %dynamic-slice_subtract_fusion), channel_id=10, replica_groups=mesh['blk'=16,'grp'=2] {'blk'}, dimensions={1}, use_global_device_ids=true | all-gather | bytes 557056 | tf_op jit(solution)/shard_map/all_gather | solution.py:25
  (49 shorter events, 15.9 us)
Async XLA Ops:
  7.2 185.7 %copy-start = (f32[8,64,1024]{2,1,0:T(8,128)S(1)}, f32[8,64,1024]{2,1,0:T(8,128)}, u32[]{:S(2)}) copy-start(f32[8,64,1024]{2,1,0:T(8,128)} %param.13) | copy-start | bytes 6291460
  7.2 146.6 %all-reduce.2.cloned.1.call-start = ((), (), s32[]{:S(2)}) async-start(), calls=%async_computation | async-start | bytes 524288 | tf_op jit(solution)/shard_map/psum | solution.py:63
  57.2 38.7 %copy-start.7 = (s32[2,24]{1,0:T(2,128)S(1)}, s32[2,24]{1,0:T(2,128)}, u32[]{:S(2)}) copy-start(s32[2,24]{1,0:T(2,128)} %param.10) | copy-start | bytes 580
  57.2 39.9 %copy-start.6 = (s32[8]{0:T(128)S(1)}, s32[8]{0:T(128)}, u32[]{:S(2)}) copy-start(s32[8]{0:T(128)} %param.11) | copy-start | bytes 100
  95.9 673.2 %copy-start.2 = (f32[2,1024,128]{2,1,0:T(8,128)}, f32[2,1024,128]{2,1,0:T(8,128)S(1)}, u32[]{:S(2)}) copy-start(f32[2,1024,128]{2,1,0:T(8,128)S(1)} %get-tuple-element.3) | copy-start | bytes 3145732
  192.9 44.9 %copy-start.5 = (f32[8,64,128]{2,1,0:T(8,128)S(1)}, f32[8,64,128]{2,1,0:T(8,128)}, u32[]{:S(2)}) copy-start(f32[8,64,128]{2,1,0:T(8,128)} %all-reduce.2.cloned.1.call-done) | copy-start | bytes 786436
  192.9 290.9 %copy-start.1 = (f32[8,8,64,1024]{3,2,1,0:T(8,128)S(1)}, f32[8,8,64,1024]{3,2,1,0:T(8,128)}, u32[]{:S(2)}) copy-start(f32[8,8,64,1024]{3,2,1,0:T(8,128)} %param.12) | copy-start | bytes 50331652
  728.5 40.8 %copy-start.3 = (f32[2,1024,128]{2,1,0:T(8,128)S(1)}, f32[2,1024,128]{2,1,0:T(8,128)}, u32[]{:S(2)}) copy-start(f32[2,1024,128]{2,1,0:T(8,128)} %param.9) | copy-start | bytes 3145732
  728.5 40.8 %copy-start.4 = (f32[2,1000,128]{2,1,0:T(8,128)S(1)}, f32[2,1000,128]{2,1,0:T(8,128)}, u32[]{:S(2)}) copy-start(f32[2,1000,128]{2,1,0:T(8,128)} %slice.42) | copy-start | bytes 3072004
Sparse Core Ops, SparseCore 0:
  97.2 18.6 all-reduce.1
